TPU v7x, 128 devices: a whole 4x4x4 slice. The times are simulated.
128 devices in a mesh: tok: 16 (over z, y_lo, core), feat: 8 (over y_hi, x).
Axes of the slice: x: 4, y: 4 (y_hi: 2, y_lo: 2; y = y_hi * 2 + y_lo), z: 4, core: 2. Of those that a mesh axis runs over, the one named last changes fastest.
Arguments:
- teacher: float32 [8192, 16384], P('tok', 'feat'), may hold values from -720 to 720, as said below
- student: float32 [8192, 2048], P('tok', 'feat'), may hold values from -6 to 6
- gain: float32 [16384], P('feat'), may hold values from 0.1 to 1.9
- projector: float32 [2048, 16384], P(None, 'feat'), may hold values from -0.1875 to 0.1875
- momentum: float32 [2048, 16384], P('tok', 'feat'), may hold values from -0.12 to 0.12
Outputs:
- new_projector: float32 [2048, 16384], P('tok', 'feat')
- new_momentum: float32 [2048, 16384], P('tok', 'feat')
- student_grad: float32 [8192, 2048], P('tok', 'feat')
- loss_value: float32 [], replicated
Inputs may be any that keep to these rules, and one draw needn't show every extreme that they name: `teacher`: finite real values.
All inputs are finite; a program needn't handle non-finite values.
Results may differ from a plain program's by a relative error of at most 0.00011.
Values sent between devices are 32-bit elements; how exact they have to be, the bound alone decides.
No kernel may reach another device: no remote copies, remote signals or barrier semaphores. Data moves between devices by JAX's collectives and lax.ppermute only.
A program may use at most 128 MiB of HBM per device.

v0:
```python
import jax
import jax.numpy as jnp
from jax import lax
from jax.sharding import Mesh
from jax.sharding import PartitionSpec as P

DT = 16384
TOK = ("tok_0", "tok_1", "tok_2")
FEAT = ("feat_0", "feat_1")
TOK_FEAT = ("tok_0", "tok_1", "tok_2", "feat_0", "feat_1")
norm_eps = 1e-05
momentum_rate = 0.9
step_rate = 0.5


def over_axes(value, axes):
    for axis in axes:
        value = lax.psum(value, axis)
    return value


def split_up(value, dim, devices):
    before, after = (value.shape[:dim], value.shape[dim + 1 :])
    return jnp.moveaxis(value.reshape(*before, devices, -1, *after), dim, 0)


def summed_on_arrival(value, axis, dim):
    blocks = split_up(value, dim, lax.axis_size(axis))
    arrived = lax.all_to_all(blocks, axis, split_axis=0, concat_axis=0, tiled=True)
    return arrived.sum(axis=0)


def on_device(teacher, student, gain, projector, momentum):
    highest = lax.Precision.HIGHEST
    local_rows = teacher.shape[0]
    token_count = local_rows * lax.axis_size(TOK)
    full_student = lax.all_gather(student, FEAT, axis=1, tiled=True)
    predicted = jnp.dot(
        full_student, projector, precision=highest, preferred_element_type=jnp.float32
    )
    weighted = teacher * gain[None, :]
    squares_part = jnp.sum(teacher * teacher, axis=1)
    row_total = lax.psum(squares_part, FEAT)
    row_scale = lax.rsqrt(row_total / DT + norm_eps)
    residual = predicted - weighted * row_scale[:, None]
    error_sum = over_axes(jnp.sum(residual * residual), TOK_FEAT)
    loss_value = error_sum / (token_count * DT)
    own_count = projector.shape[0] // lax.axis_size(TOK)
    proj_grad = lax.psum_scatter(
        lax.dot_general(
            full_student,
            residual,
            (((0,), (0,)), ((), ())),
            precision=highest,
            preferred_element_type=jnp.float32,
        )
        / token_count,
        TOK,
        scatter_dimension=0,
        tiled=True,
    )
    student_terms = lax.dot_general(
        residual,
        projector,
        (((1,), (1,)), ((), ())),
        precision=highest,
        preferred_element_type=jnp.float32,
    )
    student_grad = summed_on_arrival(student_terms, FEAT, 1)
    new_momentum = momentum_rate * momentum + proj_grad
    first_own = lax.axis_index(TOK) * own_count
    own_rows = lax.dynamic_slice_in_dim(projector, first_own, own_count, 0)
    new_projector = own_rows - step_rate * new_momentum
    return (new_projector, new_momentum, student_grad, loss_value)


def solution(mesh):
    split = Mesh(
        mesh.devices.reshape(4, 2, 2, 2, 4), ("tok_0", "tok_1", "tok_2", "feat_0", "feat_1")
    )
    in_specs = (P(TOK, FEAT), P(TOK, FEAT), P(FEAT), P(None, FEAT), P(TOK, FEAT))
    out_specs = (P(TOK, FEAT), P(TOK, FEAT), P(TOK, FEAT), P())
    return jax.shard_map(
        on_device, mesh=split, in_specs=in_specs, out_specs=out_specs, check_vma=False
    )
```

profile of v0, /device:TPU:0, one launch (start us, length us, event | category | flops | bytes accessed | tf_op | source)
XLA Modules:
  0.0 395.2 jit_solution(3353362954193325163)
XLA Ops:
  7.2 0.0 copy-start.4
  7.2 0.0 all-gather.2.cloned.1.call-start
  7.2 0.7 all-gather.2.cloned.1.call-update
  7.9 0.0 reduce-scatter.2.cloned.1.call-start
  8.0 2.5 multiply_reduce_fusion
  10.5 24.6 %psum.42 = f32[512]{0:T(512)S(1)} all-reduce(f32[512]{0:T(512)S(1)} %multiply_reduce_fusion), channel_id=1, replica_groups=mesh['tok_0'=4,'tok_1'=2,'tok_2'=2,'feat_0'=2,'feat_1'=4] {'feat_0','fea..., use_global_device_ids=true, to_apply=%region_1.0 | all-reduce | flops 512 | bytes 4096 | tf_op jit(solution)/shard_map/psum | solution.py:43
  35.1 54.8 %all-gather.2.cloned.1.call-done = f32[512,2048]{1,0:T(8,128)} async-done(((f32[512,256]{1,0:T(8,128)}), f32[512,2048]{1,0:T(8,128)}) %all-gather.2.cloned.1.call-update) | async-done | bytes 4194320 | tf_op jit(solution)/shard_map/all_gather | solution.py:37
  89.9 0.0 copy-done.4
  89.9 0.0 copy-start
  89.9 0.0 copy-start.2
  89.9 32.5 %fusion.6 = (f32[]{:T(128)}, f32[512,2048]{1,0:T(8,128)S(1)}) fusion(f32[512,2048]{1,0:T(8,128)} %param.5, f32[512]{0:T(512)S(1)} %add_rsqrt_fusion, f32[2048]{0:T(1024)S(1)} %copy-done.4, f32[512,2048]{1,0:T(8,128)} %all-gather.2.cloned.1.call-done, f32[2048,2048]{1,0:T(8,128)} %param.8), kind=kOutput, calls=%fused_computation.6 | convolution fusion | flops 25775046656 | bytes 29370372 | tf_op jit(solution)/shard_map/dot_general | solution.py:38
  122.4 0.0 copy-start.1
  122.4 1.9 copy-done.1
  124.3 0.0 copy-done
  124.3 0.0 copy-done.2
  124.3 30.1 %multiply_bitcast_fusion = f32[2048,2048]{0,1:T(8,128)} fusion(f32[512,2048]{1,0:T(8,128)S(1)} %copy-done.2, f32[512,2048]{1,0:T(8,128)S(1)} %get-tuple-element.15, f32[512,2048]{1,0:T(8,128)S(1)} %copy-done, f32[512]{0:T(512)S(1)} %add_rsqrt_fusion, f32[2048]{0:T(1024)S(1)} %copy-done.4), kind=kOutput, calls=%fused_computation | convolution fusion | flops 25777143808 | bytes 29370368 | tf_op jit(solution)/shard_map/dot_general | solution.py:50
  154.4 0.0 reduce-scatter.2.cloned.1.call-update
  154.5 32.0 %fusion = f32[512,2048]{1,0:T(8,128)S(1)} fusion(f32[2048,2048]{1,0:T(8,128)} %param.8, f32[512,2048]{1,0:T(8,128)} %copy-done.1, f32[512,2048]{1,0:T(8,128)} %param.5, f32[512]{0:T(512)S(1)} %add_rsqrt_fusion, f32[2048]{0:T(1024)S(1)} %copy-done.4), kind=kOutput, calls=%fused_computation.2 | convolution fusion | flops 25772949504 | bytes 29370368 | tf_op jit(solution)/shard_map/dot_general | solution.py:62
  186.5 2.4 copy.21
  188.8 4.5 %all-to-all-start = ((f32[8,512,256]{2,1,0:T(8,128)}), f32[8,512,256]{2,1,0:T(8,128)}, u32[]{:S(2)}, u32[]{:S(2)}) async-start(f32[8,512,256]{2,1,0:T(8,128)} %bitcast.13), calls=%async_computation.1 | async-start | bytes 8388608 | tf_op jit(solution)/shard_map/all_to_all | solution.py:29
  193.4 0.0 copy-start.3
  193.4 11.3 %psum.43 = f32[]{:T(128)} all-reduce(f32[]{:T(128)} %get-tuple-element.14), channel_id=1, replica_groups=mesh['tok_0'=4,'tok_1'=2,'tok_2'=2,'feat_0'=2,'feat_1'=4] {'tok_0'}, use_global_device_ids=true, to_apply=%region_5.0 | all-reduce | flops 1 | bytes 8 | tf_op jit(solution)/shard_map/psum | solution.py:18
  204.8 47.1 %psum.44 = f32[]{:T(128)} all-reduce(f32[]{:T(128)} %psum.43), channel_id=1, replica_groups=mesh['tok_0'=4,'tok_1'=2,'tok_2'=2,'feat_0'=2,'feat_1'=4] {'tok_1'}, use_global_device_ids=true, to_apply=%region_6.0 | all-reduce | flops 1 | bytes 8 | tf_op jit(solution)/shard_map/psum | solution.py:18
  251.9 1.3 constant_dynamic-slice_fusion
  253.2 3.1 psum.45
  256.3 0.3 copy.18
  256.6 7.8 %psum.46 = f32[]{:T(128)} all-reduce(f32[]{:T(128)} %psum.45), channel_id=1, replica_groups=mesh['tok_0'=4,'tok_1'=2,'tok_2'=2,'feat_0'=2,'feat_1'=4] {'feat_0'}, use_global_device_ids=true, to_apply=%region_8.0 | all-reduce | flops 1 | bytes 8 | tf_op jit(solution)/shard_map/psum | solution.py:18
  264.4 0.0 copy-done.3
  264.4 0.3 copy.14
  264.7 9.8 %psum.47 = f32[]{:T(128)} all-reduce(f32[]{:T(128)} %psum.46), channel_id=1, replica_groups=mesh['tok_0'=4,'tok_1'=2,'tok_2'=2,'feat_0'=2,'feat_1'=4] {'feat_1'}, use_global_device_ids=true, to_apply=%region_9.0 | all-reduce | flops 1 | bytes 8 | tf_op jit(solution)/shard_map/psum | solution.py:18
  275.2 0.0 all-to-all-done
  275.2 3.3 reduce_sum.28
  278.6 102.5 %reduce-scatter.2.cloned.1.call-done = f32[128,2048]{0,1:T(8,128)} async-done(((f32[2048,2048]{0,1:T(8,128)}), f32[128,2048]{0,1:T(8,128)}) %reduce-scatter.2.cloned.1.call-update) | async-done | bytes 1048592 | tf_op jit(solution)/shard_map/reduce_scatter | solution.py:49
  381.0 2.4 multiply_subtract_fusion
  383.4 2.5 copy.16
  385.9 1.3 copy.17
  (1 shorter events, 0.0 us)
Async XLA Ops:
  7.2 82.7 %copy-start.4 = (f32[2048]{0:T(1024)S(1)}, f32[2048]{0:T(1024)}, u32[]{:S(2)}) copy-start(f32[2048]{0:T(1024)} %param.7) | copy-start | bytes 24580
  7.2 82.7 %all-gather.2.cloned.1.call-start = ((), (), s32[]{:S(2)}) async-start(), calls=%async_computation.2 | async-start | bytes 4718592 | tf_op jit(solution)/shard_map/all_gather | solution.py:37
  7.9 373.1 %reduce-scatter.2.cloned.1.call-start = ((), (), s32[]{:S(2)}) async-start(), calls=%async_computation.3 | async-start | bytes 17825792 | tf_op jit(solution)/shard_map/reduce_scatter | solution.py:49
  89.9 34.5 %copy-start = (f32[512,2048]{1,0:T(8,128)S(1)}, f32[512,2048]{1,0:T(8,128)}, u32[]{:S(2)}) copy-start(f32[512,2048]{1,0:T(8,128)} %param.5) | copy-start | bytes 12582916
  89.9 34.5 %copy-start.2 = (f32[512,2048]{1,0:T(8,128)S(1)}, f32[512,2048]{1,0:T(8,128)}, u32[]{:S(2)}) copy-start(f32[512,2048]{1,0:T(8,128)} %all-gather.2.cloned.1.call-done) | copy-start | bytes 12582916
  122.4 1.9 copy-start.1
  188.8 86.4 %all-to-all-start = ((f32[8,512,256]{2,1,0:T(8,128)}), f32[8,512,256]{2,1,0:T(8,128)}, u32[]{:S(2)}, u32[]{:S(2)}) async-start(f32[8,512,256]{2,1,0:T(8,128)} %bitcast.13), calls=%async_computation.1 | async-start | bytes 8388608 | tf_op jit(solution)/shard_map/all_to_all | solution.py:29
  193.4 71.0 %copy-start.3 = (f32[128,2048]{1,0:T(8,128)S(1)}, f32[128,2048]{1,0:T(8,128)}, u32[]{:S(2)}) copy-start(f32[128,2048]{1,0:T(8,128)} %param.9) | copy-start | bytes 3145732
Sparse Core Ops, SparseCore 0:
  10.2 79.6 all-gather.1
  154.6 226.3 reduce-scatter.1
where the time goes:
time: 396 us; the launch traced here: 395 us
  waiting for transfers between devices  158 us (40%)
  blocking collectives  104 us (26%)
  matrix products  94.6 us (24%)
  between operations  15.9 us (4%)
  local copies, waits for them, and re-layouts  10.1 us (3%)
  other arithmetic  8.28 us (2%)
  starting transfers between devices  4.62 us (1%)
    reduce_scatter x1, waiting for transfers between devices, on_device(): lax.psum_scatter(lax.dot_general(full_student, residual, (((0,), (0,)), (...  102 us
    psum x5, blocking collectives, over_axes(): value = lax.psum(value, axis)  79.2 us
    all_gather x1, waiting for transfers between devices, on_device(): full_student = lax.all_gather(student, FEAT, axis=1, tiled=True)  54.8 us
    dot_general x1, matrix products, on_device(): jnp.dot(full_student, projector, precision=highest, preferred_element_typ...  32.5 us
    dot_general x1, matrix products, on_device(): lax.dot_general(residual, projector, (((1,), (1,)), ((), ())), precision=...  32 us
    dot_general x1, matrix products, on_device(): lax.dot_general(full_student, residual, (((0,), (0,)), ((), ())), precisi...  30.1 us
    psum x1, blocking collectives, on_device(): row_total = lax.psum(squares_part, FEAT)  24.6 us
  transfers between devices with their start and end apart: 3, of which 2 were waited for; matrix products, arithmetic and copies ran while one was open for 11% of the time, Pallas kernels for 0%

commit v1 on v0

--- a/solution.py
+++ b/solution.py
@@ -11,6 +11,9 @@
 norm_eps = 1e-05
 momentum_rate = 0.9
 step_rate = 0.5
+_render_runs = lambda block_here: lax.psum(
+    lax.psum(block_here, axis_name="feat_1"), axis_name="feat_0"
+)
 
 
 def over_axes(value, axes):
@@ -40,7 +43,7 @@
     )
     weighted = teacher * gain[None, :]
     squares_part = jnp.sum(teacher * teacher, axis=1)
-    row_total = lax.psum(squares_part, FEAT)
+    row_total = _render_runs(squares_part)
     row_scale = lax.rsqrt(row_total / DT + norm_eps)
     residual = predicted - weighted * row_scale[:, None]
     error_sum = over_axes(jnp.sum(residual * residual), TOK_FEAT)

time: 396 us -> 396 us (level)
  blocking collectives: 104 us -> 96.2 us
  waiting for transfers between devices: 158 us -> 165 us
    psum x1 -> x2, blocking collectives: 24.6 us -> 17 us  [the longest x1 10.6 us: lax.psum(block_here, axis_name='feat_1')]
    all_gather x1, waiting for transfers between devices: 54.8 us -> 62.3 us  [on_device(): full_student = lax.all_gather(student, FEAT, axis=1, tiled=True)]
where the time goes in v1:
time: 396 us; the launch traced here: 395 us
  waiting for transfers between devices  165 us (42%)
  blocking collectives  96.2 us (24%)
  matrix products  94.6 us (24%)
  between operations  15.9 us (4%)
  local copies, waits for them, and re-layouts  10.1 us (3%)
  other arithmetic  8.28 us (2%)
  starting transfers between devices  4.62 us (1%)
    reduce_scatter x1, waiting for transfers between devices, on_device(): lax.psum_scatter(lax.dot_general(full_student, residual, (((0,), (0,)), (...  102 us
    psum x5, blocking collectives, over_axes(): value = lax.psum(value, axis)  79.2 us
    all_gather x1, waiting for transfers between devices, on_device(): full_student = lax.all_gather(student, FEAT, axis=1, tiled=True)  62.3 us
    dot_general x1, matrix products, on_device(): jnp.dot(full_student, projector, precision=highest, preferred_element_typ...  32.5 us
    dot_general x1, matrix products, on_device(): lax.dot_general(residual, projector, (((1,), (1,)), ((), ())), precision=...  32 us
    dot_general x1, matrix products, on_device(): lax.dot_general(full_student, residual, (((0,), (0,)), ((), ())), precisi...  30.1 us
    psum x1, blocking collectives, lax.psum(block_here, axis_name='feat_1')  10.6 us
  transfers between devices with their start and end apart: 3, of which 2 were waited for; matrix products, arithmetic and copies ran while one was open for 11% of the time, Pallas kernels for 0%

profile of v1, /device:TPU:0, one launch (start us, length us, event | category | flops | bytes accessed | tf_op | source)
XLA Modules:
  0.0 395.1 jit_solution(377545476042672960)
XLA Ops:
  7.2 0.0 copy-start.4
  7.2 0.0 all-gather.2.cloned.1.call-start
  7.2 0.7 all-gather.2.cloned.1.call-update
  7.9 0.0 reduce-scatter.2.cloned.1.call-start
  8.0 2.5 multiply_reduce_fusion
  10.5 10.6 %psum.49 = f32[512]{0:T(512)S(1)} all-reduce(f32[512]{0:T(512)S(1)} %multiply_reduce_fusion), channel_id=1, replica_groups=mesh['tok_0'=4,'tok_1'=2,'tok_2'=2,'feat_0'=2,'feat_1'=4] {'feat_1'}, use_global_device_ids=true, to_apply=%region_1.0 | all-reduce | flops 512 | bytes 4096 | tf_op jit(solution)/shard_map/psum | solution.py:15
  21.1 6.4 %psum.50 = f32[512]{0:T(512)S(1)} all-reduce(f32[512]{0:T(512)S(1)} %psum.49), channel_id=1, replica_groups=mesh['tok_0'=4,'tok_1'=2,'tok_2'=2,'feat_0'=2,'feat_1'=4] {'feat_0'}, use_global_device_ids=true, to_apply=%region_2.0 | all-reduce | flops 512 | bytes 4096 | tf_op jit(solution)/shard_map/psum | solution.py:14
  27.5 62.3 %all-gather.2.cloned.1.call-done = f32[512,2048]{1,0:T(8,128)} async-done(((f32[512,256]{1,0:T(8,128)}), f32[512,2048]{1,0:T(8,128)}) %all-gather.2.cloned.1.call-update) | async-done | bytes 4194320 | tf_op jit(solution)/shard_map/all_gather | solution.py:40
  89.8 0.0 copy-done.4
  89.8 0.0 copy-start
  89.8 0.0 copy-start.2
  89.8 32.5 %fusion.6 = (f32[]{:T(128)}, f32[512,2048]{1,0:T(8,128)S(1)}) fusion(f32[512,2048]{1,0:T(8,128)} %param.5, f32[512]{0:T(512)S(1)} %add_rsqrt_fusion, f32[2048]{0:T(1024)S(1)} %copy-done.4, f32[512,2048]{1,0:T(8,128)} %all-gather.2.cloned.1.call-done, f32[2048,2048]{1,0:T(8,128)} %param.8), kind=kOutput, calls=%fused_computation.6 | convolution fusion | flops 25775046656 | bytes 29370372 | tf_op jit(solution)/shard_map/dot_general | solution.py:41
  122.3 0.0 copy-start.1
  122.3 1.9 copy-done.1
  124.2 0.0 copy-done
  124.2 0.0 copy-done.2
  124.3 30.1 %multiply_bitcast_fusion = f32[2048,2048]{0,1:T(8,128)} fusion(f32[512,2048]{1,0:T(8,128)S(1)} %copy-done.2, f32[512,2048]{1,0:T(8,128)S(1)} %get-tuple-element.15, f32[512,2048]{1,0:T(8,128)S(1)} %copy-done, f32[512]{0:T(512)S(1)} %add_rsqrt_fusion, f32[2048]{0:T(1024)S(1)} %copy-done.4), kind=kOutput, calls=%fused_computation | convolution fusion | flops 25777143808 | bytes 29370368 | tf_op jit(solution)/shard_map/dot_general | solution.py:53
  154.4 0.0 reduce-scatter.2.cloned.1.call-update
  154.4 32.0 %fusion = f32[512,2048]{1,0:T(8,128)S(1)} fusion(f32[2048,2048]{1,0:T(8,128)} %param.8, f32[512,2048]{1,0:T(8,128)} %copy-done.1, f32[512,2048]{1,0:T(8,128)} %param.5, f32[512]{0:T(512)S(1)} %add_rsqrt_fusion, f32[2048]{0:T(1024)S(1)} %copy-done.4), kind=kOutput, calls=%fused_computation.2 | convolution fusion | flops 25772949504 | bytes 29370368 | tf_op jit(solution)/shard_map/dot_general | solution.py:65
  186.4 2.4 copy.21
  188.7 4.5 %all-to-all-start = ((f32[8,512,256]{2,1,0:T(8,128)}), f32[8,512,256]{2,1,0:T(8,128)}, u32[]{:S(2)}, u32[]{:S(2)}) async-start(f32[8,512,256]{2,1,0:T(8,128)} %bitcast.13), calls=%async_computation.1 | async-start | bytes 8388608 | tf_op jit(solution)/shard_map/all_to_all | solution.py:32
  193.3 0.0 copy-start.3
  193.3 11.4 %psum.51 = f32[]{:T(128)} all-reduce(f32[]{:T(128)} %get-tuple-element.14), channel_id=1, replica_groups=mesh['tok_0'=4,'tok_1'=2,'tok_2'=2,'feat_0'=2,'feat_1'=4] {'tok_0'}, use_global_device_ids=true, to_apply=%region_6.0 | all-reduce | flops 1 | bytes 8 | tf_op jit(solution)/shard_map/psum | solution.py:21
  204.7 47.1 %psum.52 = f32[]{:T(128)} all-reduce(f32[]{:T(128)} %psum.51), channel_id=1, replica_groups=mesh['tok_0'=4,'tok_1'=2,'tok_2'=2,'feat_0'=2,'feat_1'=4] {'tok_1'}, use_global_device_ids=true, to_apply=%region_7.0 | all-reduce | flops 1 | bytes 8 | tf_op jit(solution)/shard_map/psum | solution.py:21
  251.8 1.3 constant_dynamic-slice_fusion
  253.1 3.1 psum.53
  256.2 0.3 copy.18
  256.5 7.8 %psum.54 = f32[]{:T(128)} all-reduce(f32[]{:T(128)} %psum.53), channel_id=1, replica_groups=mesh['tok_0'=4,'tok_1'=2,'tok_2'=2,'feat_0'=2,'feat_1'=4] {'feat_0'}, use_global_device_ids=true, to_apply=%region_9.0 | all-reduce | flops 1 | bytes 8 | tf_op jit(solution)/shard_map/psum | solution.py:21
  264.3 0.0 copy-done.3
  264.3 0.3 copy.14
  264.6 9.8 %psum.55 = f32[]{:T(128)} all-reduce(f32[]{:T(128)} %psum.54), channel_id=1, replica_groups=mesh['tok_0'=4,'tok_1'=2,'tok_2'=2,'feat_0'=2,'feat_1'=4] {'feat_1'}, use_global_device_ids=true, to_apply=%region_10.0 | all-reduce | flops 1 | bytes 8 | tf_op jit(solution)/shard_map/psum | solution.py:21
  275.1 0.0 all-to-all-done
  275.1 3.3 reduce_sum.28
  278.5 102.5 %reduce-scatter.2.cloned.1.call-done = f32[128,2048]{0,1:T(8,128)} async-done(((f32[2048,2048]{0,1:T(8,128)}), f32[128,2048]{0,1:T(8,128)}) %reduce-scatter.2.cloned.1.call-update) | async-done | bytes 1048592 | tf_op jit(solution)/shard_map/reduce_scatter | solution.py:52
  380.9 2.4 multiply_subtract_fusion
  383.3 2.5 copy.16
  385.8 1.3 copy.17
  (1 shorter events, 0.0 us)
Async XLA Ops:
  7.2 82.6 %copy-start.4 = (f32[2048]{0:T(1024)S(1)}, f32[2048]{0:T(1024)}, u32[]{:S(2)}) copy-start(f32[2048]{0:T(1024)} %param.7) | copy-start | bytes 24580
  7.2 82.6 %all-gather.2.cloned.1.call-start = ((), (), s32[]{:S(2)}) async-start(), calls=%async_computation.2 | async-start | bytes 4718592 | tf_op jit(solution)/shard_map/all_gather | solution.py:40
  7.9 373.0 %reduce-scatter.2.cloned.1.call-start = ((), (), s32[]{:S(2)}) async-start(), calls=%async_computation.3 | async-start | bytes 17825792 | tf_op jit(solution)/shard_map/reduce_scatter | solution.py:52
  89.8 34.5 %copy-start = (f32[512,2048]{1,0:T(8,128)S(1)}, f32[512,2048]{1,0:T(8,128)}, u32[]{:S(2)}) copy-start(f32[512,2048]{1,0:T(8,128)} %param.5) | copy-start | bytes 12582916
  89.8 34.5 %copy-start.2 = (f32[512,2048]{1,0:T(8,128)S(1)}, f32[512,2048]{1,0:T(8,128)}, u32[]{:S(2)}) copy-start(f32[512,2048]{1,0:T(8,128)} %all-gather.2.cloned.1.call-done) | copy-start | bytes 12582916
  122.3 1.9 copy-start.1
  188.7 86.4 %all-to-all-start = ((f32[8,512,256]{2,1,0:T(8,128)}), f32[8,512,256]{2,1,0:T(8,128)}, u32[]{:S(2)}, u32[]{:S(2)}) async-start(f32[8,512,256]{2,1,0:T(8,128)} %bitcast.13), calls=%async_computation.1 | async-start | bytes 8388608 | tf_op jit(solution)/shard_map/all_to_all | solution.py:32
  193.3 71.0 %copy-start.3 = (f32[128,2048]{1,0:T(8,128)S(1)}, f32[128,2048]{1,0:T(8,128)}, u32[]{:S(2)}) copy-start(f32[128,2048]{1,0:T(8,128)} %param.9) | copy-start | bytes 3145732
Sparse Core Ops, SparseCore 0:
  10.2 79.5 all-gather.1
  154.5 226.3 reduce-scatter.1
